TPU v7x, 32 devices: a whole 2x2x4 slice. The times are simulated.
32 devices in a mesh: row: 8 (over z, y), col: 4 (over x, core).
Axes of the slice: x: 2, y: 2, z: 4, core: 2. Of those that a mesh axis runs over, the one named last changes fastest.
Arguments:
- tensor: bfloat16 [1024, 64, 512], P('row', None, 'col'), may hold values from -6 to 6
- loss_kind: int32 [1024, 64, 512], P('row', None, 'col'), may hold values from 0 to 1, as said below
- factor_one: float32 [1024, 512], P(('row', 'col')), may hold values from -2 to 2
- factor_two: float32 [512, 512], P(('col', 'row')), may hold values from -2 to 2
- factor_three: float32 [64, 512], replicated, may hold values from -2 to 2
- first_one: float32 [1024, 512], P(('row', 'col')), may hold values from -0.03 to 0.03
- second_one: float32 [1024, 512], P(('row', 'col')), may hold values from 0.0005 to 0.05
- first_two: float32 [512, 512], P(('col', 'row')), may hold values from -0.03 to 0.03
- second_two: float32 [512, 512], P(('col', 'row')), may hold values from 0.0005 to 0.05
- first_three: float32 [64, 512], replicated, may hold values from -0.03 to 0.03
- second_three: float32 [64, 512], replicated, may hold values from 0.0005 to 0.05
Outputs:
- new_one: float32 [1024, 512], P(('row', 'col'))
- new_two: float32 [512, 512], P(('col', 'row'))
- new_three: float32 [64, 512], replicated
Inputs may be any that keep to these rules, and one draw needn't show every extreme that they name: loss_kind takes one value on each block of 128 first-mode by 128 second-mode indices (with all 64 third-mode ones), aligned to multiples of 128 and 128, and is 1 on exactly half of these blocks.
All inputs are finite; a program needn't handle non-finite values.
Results may differ from a plain program's by a relative error of at most 0.003.
Values may be sent and summed in bfloat16 or wider, within the bound.
A program may use at most 128 MiB of HBM per device.

v0:
```python
import functools
import math

import jax
import jax.numpy as jnp
from jax import lax
from jax.experimental import pallas as pl
from jax.experimental.pallas import tpu as pltpu
from jax.sharding import PartitionSpec as P

ITERS = 2
STEP = 10
BLOCK = 32
LANES = 128

learn_rate = 0.05
beta_one = 0.8
beta_two = 0.95
adam_eps = 1e-08

F32 = jnp.float32
BF16 = jnp.bfloat16


def adam_step(param, first, second, grad, counter):
    first = beta_one * first + (1.0 - beta_one) * grad
    second = beta_two * second + (1.0 - beta_two) * grad * grad
    corr_one = 1.0 - beta_one**counter
    corr_two = 1.0 - beta_two**counter
    param = param - learn_rate * (first / corr_one) / (jnp.sqrt(second / corr_two) + adam_eps)
    return (param, first, second)


def kernel(
    n_row, n_col, scales,
    tensor, kind, a_hbm, b_hbm, c_hbm, ma_hbm, va_hbm, mb_hbm, vb_hbm, mc_hbm, vc_hbm,
    oa, ob, oc,
    x_s, kind_s, ag_a, ag_b, ag_c, gs_a, gs_b, gs_c, rs_a, rs_b, rs_c,
    a_f, bt, c_f, ga, gb, gc, st_a, st_b, st_c, split, p_s, y_s,
    a_in, b_in, c_in, ma_in, va_in, mb_in, vb_in, mc_in, vc_in,
    load_sem, sends, recvs,
):
    row = lax.axis_index("row")
    col = lax.axis_index("col")
    n_all = n_row * n_col
    me = row * n_col + col
    tile_rows, depth, tile_cols = x_s.shape
    rank = a_f.shape[1]
    own_a = a_in.shape[0]
    own_b = b_in.shape[0]
    step_rows = min(BLOCK, own_a)
    second_rows = BLOCK * depth
    chunk = st_c.shape[1]
    groups = rank // LANES

    load_x = pltpu.make_async_copy(tensor, x_s, load_sem.at[0])
    load_k = pltpu.make_async_copy(kind.at[0, pl.ds(0, 8)], kind_s, load_sem.at[1])

    pairs = (
        (a_hbm, a_in), (b_hbm, b_in), (c_hbm, c_in), (ma_hbm, ma_in), (va_hbm, va_in),
        (mb_hbm, mb_in), (vb_hbm, vb_in), (mc_hbm, mc_in), (vc_hbm, vc_in),
    )
    loads = [
        pltpu.make_async_copy(src, dst, load_sem.at[2 + i]) for i, (src, dst) in enumerate(pairs)
    ]
    for load in loads:
        load.start()
    load_k.start()
    load_x.start()

    barrier = pltpu.get_barrier_semaphore()

    def device(d):
        return {"row": lax.div(d, n_col), "col": lax.rem(d, n_col)}

    def greet(k, carry):
        pl.semaphore_signal(
            barrier, inc=1, device_id=device(lax.rem(me + k, n_all)),
            device_id_type=pl.DeviceIdType.MESH,
        )
        return carry

    lax.fori_loop(1, n_all, greet, 0)

    kinds = {
        "a": (n_col, col, lambda d: {"col": d}, 0),
        "b": (n_row, row, lambda d: {"row": d}, 1),
        "c": (n_all, me, device, 2),
    }

    def copy(src, dst, what, slot, target):
        return pltpu.make_async_remote_copy(
            src_ref=src, dst_ref=dst, send_sem=sends.at[slot], recv_sem=recvs.at[slot],
            device_id=kinds[what][2](target), device_id_type=pl.DeviceIdType.MESH,
        )

    def slot_of(what, it, phase):
        return (kinds[what][3] * 2 + phase) * (ITERS + 1) + it

    def send_all(what, it, phase, src, dst):
        n, mine, _, _ = kinds[what]

        def body(k, carry):
            peer = lax.rem(mine + k, n)
            source = src.at[it, mine] if phase == 0 else src.at[it, peer]
            copy(source, dst.at[it, mine], what, slot_of(what, it, phase), peer).start()
            return carry

        lax.fori_loop(1, n, body, 0)

    def whole(what, it, phase, src, dst):
        n, mine, _, _ = kinds[what]
        part = pl.ds(0, n - 1)
        return copy(
            src.at[it, part], dst.at[it, part], what, slot_of(what, it, phase),
            lax.rem(mine + 1, n),
        )

    started = []

    def start(what, it, phase, src, dst):
        send_all(what, it, phase, src, dst)
        started.append((what, it, phase, src, dst))

    for load in loads:
        load.wait()
    for i, ref in enumerate((c_in, mc_in, vc_in)):
        for d in range(n_all):
            g, h = d // groups, d % groups
            split[i, d] = ref[g * chunk : (g + 1) * chunk, h * LANES : (h + 1) * LANES]

    a = a_in[...]
    b = b_in[...]
    st_a[0], st_a[1], st_a[2] = a, ma_in[...], va_in[...]
    st_b[0], st_b[1], st_b[2] = b, mb_in[...], vb_in[...]
    st_c[0], st_c[1], st_c[2] = split[0, me], split[1, me], split[2, me]
    ag_a[0, col] = a.astype(BF16)
    ag_b[0, row] = b.astype(BF16)
    c_f[...] = c_in[...].astype(BF16).astype(F32)

    pl.semaphore_wait(barrier, n_all - 1)
    start("b", 0, 0, ag_b, ag_b)
    start("a", 0, 0, ag_a, ag_a)
    load_x.wait()
    load_k.wait()

    spread = learn_rate * ITERS
    for it in range(ITERS):
        whole("a", it, 0, ag_a, ag_a).wait_recv()
        whole("b", it, 0, ag_b, ag_b).wait_recv()
        if it > 0:
            whole("c", it, 0, ag_c, ag_c).wait_recv()
            for d in range(n_all):
                g, h = d // groups, d % groups
                c_f[g * chunk : (g + 1) * chunk, h * LANES : (h + 1) * LANES] = (
                    ag_c[it, d].astype(BF16).astype(F32)
                )
        a_f[...] = ag_a[it].reshape(tile_rows, rank).astype(F32)
        bt[...] = ag_b[it].reshape(tile_cols, rank).T
        gb[...] = jnp.zeros_like(gb)
        gc[...] = jnp.zeros_like(gc)

        def owner(t, carry):
            q = lax.rem(col + 1 + t, n_col)
            base = pl.multiple_of(q * own_a, own_a)

            def block(s, carry):
                at = pl.ds(pl.multiple_of(base + s * step_rows, step_rows), step_rows)
                a8 = a_f[at, :]
                c3 = c_f[...]
                p = (a8[:, None, :] * c3[None]).astype(BF16).reshape(step_rows * depth, rank)
                span = pl.ds(
                    pl.multiple_of((base + s * step_rows) * depth, step_rows * depth), step_rows * depth
                )
                p_s[span, :] = p
                m = jnp.dot(p, bt[...], preferred_element_type=F32)
                x = x_s[at].reshape(step_rows * depth, tile_cols).astype(F32)
                huber = jnp.clip(m - x, -1.0, 1.0)
                logit = 0.5 * jnp.tanh(0.5 * m) + jnp.where(x > 0, -0.5, 0.5)
                is_logit = jnp.broadcast_to(kind_s[0:1, :], m.shape) == 1
                y = jnp.where(is_logit, logit, huber).astype(BF16)
                z = jnp.dot(
                    y, ag_b[it].reshape(tile_cols, rank), preferred_element_type=F32
                ).reshape(step_rows, depth, rank)
                ga[at, :] = jnp.sum(z * c3[None], axis=1) * scales[0]
                gc[...] += jnp.sum(z * a8[:, None, :], axis=0)
                y_s[span, :] = y
                return carry

            lax.fori_loop(0, own_a // step_rows, block, 0)
            gs_a[it, q] = ga[pl.ds(base, own_a), :].astype(BF16)

            @pl.when(t < n_col - 1)
            def _():
                copy(gs_a.at[it, q], rs_a.at[it, col], "a", slot_of("a", it, 1), q).start()

            return carry

        lax.fori_loop(0, n_col, owner, 0)
        started.append(("a", it, 1, gs_a, rs_a))

        for d in range(n_all):
            g, h = d // groups, d % groups
            gs_c[it, d] = (
                gc[g * chunk : (g + 1) * chunk, h * LANES : (h + 1) * LANES] * scales[2]
            ).astype(BF16)
        start("c", it, 1, gs_c, rs_c)
        rs_c[it, me] = gs_c[it, me]

        def second(s, carry):
            span = pl.ds(pl.multiple_of(s * second_rows, second_rows), second_rows)
            gb[...] += lax.dot_general(
                y_s[span, :], p_s[span, :], (((0,), (0,)), ((), ())), preferred_element_type=F32
            )
            return carry

        lax.fori_loop(0, tile_rows * depth // second_rows, second, 0)
        gb[...] = gb[...] * scales[1]
        gs_b[it] = gb[...].astype(BF16).reshape(n_row, own_b, rank)
        start("b", it, 1, gs_b, rs_b)

        counter = STEP + it + 1
        last = it == ITERS - 1

        def apply(state, grad):
            f, m, v = adam_step(state[0], state[1], state[2], grad, counter)
            state[0], state[1], state[2] = f, m, v
            return f

        whole("a", it, 1, gs_a, rs_a).wait_recv()
        grad = ga[pl.ds(pl.multiple_of(col * own_a, own_a), own_a), :]
        for k in range(1, n_col):
            grad = grad + rs_a[it, lax.rem(col + k, n_col)].astype(F32)
        a = apply(st_a, grad)
        if last:
            oa[...] = (a_in[...] - a) / spread
        else:
            ag_a[it + 1, col] = a.astype(BF16)
            start("a", it + 1, 0, ag_a, ag_a)

        whole("c", it, 1, gs_c, rs_c).wait_recv()
        c = apply(st_c, jnp.sum(rs_c[it].astype(F32), axis=0))
        ag_c[it + 1, me] = (split[0, me] - c) / spread if last else c
        start("c", it + 1, 0, ag_c, ag_c)

        whole("b", it, 1, gs_b, rs_b).wait_recv()
        grad = gb[pl.ds(pl.multiple_of(row * own_b, own_b), own_b), :]
        for k in range(1, n_row):
            grad = grad + rs_b[it, lax.rem(row + k, n_row)].astype(F32)
        b = apply(st_b, grad)
        if last:
            ob[...] = (b_in[...] - b) / spread
        else:
            ag_b[it + 1, row] = b.astype(BF16)
            start("b", it + 1, 0, ag_b, ag_b)

    whole("c", ITERS, 0, ag_c, ag_c).wait_recv()
    for d in range(n_all):
        g, h = d // groups, d % groups
        oc[g * chunk : (g + 1) * chunk, h * LANES : (h + 1) * LANES] = ag_c[ITERS, d]
    for args in started:
        whole(*args).wait_send()


def hand_on(a, b, c, oa, ob, oc):
    oa[...] = a[...]
    ob[...] = b[...]
    oc[...] = c[...]


def shards(tensor, loss_kind, a, b, c, ma, va, mb, vb, mc, vc):
    tile_rows, depth, tile_cols = tensor.shape
    rank = a.shape[1]
    n_row = lax.axis_size("row")
    n_col = lax.axis_size("col")
    n_all = n_row * n_col
    full_rows = tile_rows * n_row
    full_cols = tile_cols * n_col
    scales = (
        1.0 / math.sqrt(full_cols * depth),
        1.0 / math.sqrt(full_rows * depth),
        1.0 / math.sqrt(full_rows * full_cols),
    )
    chunk = depth * rank // (n_all * LANES)
    own_a, own_b = a.shape[0], b.shape[0]
    vmem = pl.BlockSpec(memory_space=pltpu.VMEM)
    hbm = pl.BlockSpec(memory_space=pl.ANY)
    slots = 6 * (ITERS + 1)
    outs = pl.pallas_call(
        functools.partial(kernel, n_row, n_col, scales),
        out_shape=tuple(jax.ShapeDtypeStruct(f.shape, F32) for f in (a, b, c)),
        in_specs=[hbm] * 11,
        out_specs=[vmem] * 3,
        scratch_shapes=[
            pltpu.VMEM(tensor.shape, tensor.dtype),
            pltpu.VMEM((8, tile_cols), jnp.int32),
            pltpu.VMEM((ITERS, n_col, own_a, rank), BF16),
            pltpu.VMEM((ITERS, n_row, own_b, rank), BF16),
            pltpu.VMEM((ITERS + 1, n_all, chunk, LANES), F32),
            pltpu.VMEM((ITERS, n_col, own_a, rank), BF16),
            pltpu.VMEM((ITERS, n_row, own_b, rank), BF16),
            pltpu.VMEM((ITERS, n_all, chunk, LANES), BF16),
            pltpu.VMEM((ITERS, n_col, own_a, rank), BF16),
            pltpu.VMEM((ITERS, n_row, own_b, rank), BF16),
            pltpu.VMEM((ITERS, n_all, chunk, LANES), BF16),
            pltpu.VMEM((tile_rows, rank), F32),
            pltpu.VMEM((rank, tile_cols), BF16),
            pltpu.VMEM((depth, rank), F32),
            pltpu.VMEM((tile_rows, rank), F32),
            pltpu.VMEM((tile_cols, rank), F32),
            pltpu.VMEM((depth, rank), F32),
            pltpu.VMEM((3, own_a, rank), F32),
            pltpu.VMEM((3, own_b, rank), F32),
            pltpu.VMEM((3, chunk, LANES), F32),
            pltpu.VMEM((3, n_all, chunk, LANES), F32),
            pltpu.VMEM((tile_rows * depth, rank), BF16),
            pltpu.VMEM((tile_rows * depth, tile_cols), BF16),
            *[pltpu.VMEM(f.shape, F32) for f in (a, b, c, ma, va, mb, vb, mc, vc)],
            pltpu.SemaphoreType.DMA((11,)),
            pltpu.SemaphoreType.DMA((slots,)),
            pltpu.SemaphoreType.DMA((slots,)),
        ],
        compiler_params=pltpu.CompilerParams(
            collective_id=0, has_side_effects=True, vmem_limit_bytes=60 * 1024 * 1024
        ),
    )(tensor, loss_kind, a, b, c, ma, va, mb, vb, mc, vc)
    return pl.pallas_call(
        hand_on,
        out_shape=tuple(jax.ShapeDtypeStruct(f.shape, F32) for f in (a, b, c)),
        in_specs=[vmem] * 3,
        out_specs=[vmem] * 3,
    )(*outs)


def solution(mesh):
    in_specs = (
        P("row", None, "col"),
        P("row", None, "col"),
        P(("row", "col"), None),
        P(("col", "row"), None),
        P(),
        P(("row", "col"), None),
        P(("row", "col"), None),
        P(("col", "row"), None),
        P(("col", "row"), None),
        P(),
        P(),
    )
    out_specs = (P(("row", "col"), None), P(("col", "row"), None), P())
    return jax.shard_map(shards, mesh=mesh, in_specs=in_specs, out_specs=out_specs, check_vma=False)
```

profile of v0, /device:TPU:0, one launch (start us, length us, event | category | flops | bytes accessed | tf_op | source)
XLA Modules:
  0.0 54.6 jit_solution(3492931410007918595)
XLA Ops:
  0.6 52.3 %shard_map.130 = (f32[32,512]{1,0:T(8,128)}, f32[16,512]{1,0:T(8,128)}, f32[64,512]{1,0:T(8,128)}) custom-call(bf16[128,64,128]{2,1,0:T(8,128)(2,1)} %tensor.1, s32[128,64,128]{2,1,0:T(8,128)} %kind.1, f32[32,512]{1,0:T(8,128)} %a_hbm.1, f32[16,512]{1,0:T(8,128)} %b_hbm.1, f32[64,512]{1,0:T(8,128)} %c_hbm.1, f32[32,512]{1,0:T(8,128)} %ma_hbm.1, ...), custom_call_target="tpu_custom_call" | custom-call | tf_op jit(solution)/shard_map/pallas_call | solution.py:289
  52.9 1.7 %shard_map.131 = (f32[32,512]{1,0:T(8,128)}, f32[16,512]{1,0:T(8,128)}, f32[64,512]{1,0:T(8,128)}) custom-call(f32[32,512]{1,0:T(8,128)} %get-tuple-element.6.a, f32[16,512]{1,0:T(8,128)} %get-tuple-element.7.b, f32[64,512]{1,0:T(8,128)} %get-tuple-element.8.c), custom_call_target="tpu_custom_call" | custom-call | tf_op jit(solution)/shard_map/pallas_call | solution.py:327
where the time goes:
time: 54.7 us; the launch traced here: 54.6 us
  Pallas kernels  53.9 us (99%)
  between operations  0.64 us (1%)
    pallas_call x1, Pallas kernels, shards(): pl.pallas_call(functools.partial(kernel, n_row, n_col, scales), out_shape...  52.3 us
    pallas_call x1, Pallas kernels, shards(): pl.pallas_call(hand_on, out_shape=tuple((jax.ShapeDtypeStruct(f.shape, F3...  1.65 us

commit v1 on v0

v1 whole, which is shorter than its diff:
```python
import functools
import math

import jax
import jax.numpy as jnp
from jax import lax
from jax.experimental import pallas as pl
from jax.experimental.pallas import tpu as pltpu
from jax.sharding import PartitionSpec as P

ITERS = 2
STEP = 10
HALVES = 2
P_ROWS = 16
Z_ROWS = 64
LANES = 128

learn_rate = 0.05
beta_one = 0.8
beta_two = 0.95
adam_eps = 1e-08

F32 = jnp.float32
BF16 = jnp.bfloat16


def adam_step(param, first, second, grad, counter):
    first = beta_one * first + (1.0 - beta_one) * grad
    second = beta_two * second + (1.0 - beta_two) * grad * grad
    corr_one = 1.0 - beta_one**counter
    corr_two = 1.0 - beta_two**counter
    param = param - learn_rate * (first / corr_one) / (jnp.sqrt(second / corr_two) + adam_eps)
    return (param, first, second)


def kernel(
    n_row, n_col, scales,
    tensor, kind, a_hbm, b_hbm, c_hbm, ma_hbm, va_hbm, mb_hbm, vb_hbm, mc_hbm, vc_hbm,
    oa, ob, oc,
    x_s, kind_s, ag_a, ag_b, ag_bh, ag_c, gs_a, gs_b, gs_c, rs_a, rs_b, rs_c,
    a_b, a_f, c_b, c_f, ga, gb, gc, st_a, st_b, st_c, split, p_s, y_s, m_s, out_a, out_b, out_c,
    a_in, b_in, c_in, ma_in, va_in, mb_in, vb_in, mc_in, vc_in,
    load_sem, sends, recvs, out_sem,
):
    row = lax.axis_index("row")
    col = lax.axis_index("col")
    n_all = n_row * n_col
    me = row * n_col + col
    tile_rows, depth, tile_cols = x_s.shape
    rank = a_f.shape[1]
    half = rank // HALVES
    own_a = a_in.shape[0]
    own_b = b_in.shape[0]
    chunk = st_c.shape[1]
    groups = rank // LANES

    load_x = pltpu.make_async_copy(tensor, x_s, load_sem.at[0])
    load_k = pltpu.make_async_copy(kind.at[0, pl.ds(0, 8)], kind_s, load_sem.at[1])

    pairs = (
        (a_hbm, a_in), (b_hbm, b_in), (c_hbm, c_in), (ma_hbm, ma_in), (va_hbm, va_in),
        (mb_hbm, mb_in), (vb_hbm, vb_in), (mc_hbm, mc_in), (vc_hbm, vc_in),
    )
    loads = [
        pltpu.make_async_copy(src, dst, load_sem.at[2 + i]) for i, (src, dst) in enumerate(pairs)
    ]

    def device(d):
        return {"row": lax.div(d, n_col), "col": lax.rem(d, n_col)}

    kinds = {
        "a": (n_col, col, lambda d: {"col": d}),
        "b": (n_row, row, lambda d: {"row": d}),
        "c": (n_all, me, device),
    }
    barrier = pltpu.get_barrier_semaphore()

    for what in "ba":
        n, mine, target = kinds[what]

        def greet(k, carry):
            pl.semaphore_signal(
                barrier, inc=1, device_id=target(lax.rem(mine + k, n)),
                device_id_type=pl.DeviceIdType.MESH,
            )
            return carry

        lax.fori_loop(1, n, greet, 0)

    for load in loads:
        load.start()
    load_k.start()
    load_x.start()

    slots = {}

    def copy(src, dst, what, slot, target):
        return pltpu.make_async_remote_copy(
            src_ref=src, dst_ref=dst, send_sem=sends.at[slot], recv_sem=recvs.at[slot],
            device_id=kinds[what][2](target), device_id_type=pl.DeviceIdType.MESH,
        )

    def start(what, key, scatter, src, dst):
        slot = slots[what, key, scatter] = len(slots)
        n, mine, _ = kinds[what]

        def body(k, carry):
            peer = lax.rem(mine + k, n)
            copy(src.at[peer if scatter else mine], dst.at[mine], what, slot, peer).start()
            return carry

        lax.fori_loop(1, n, body, 0)
        started.append((what, key, scatter, src, dst))

    def whole(what, key, scatter, src, dst):
        n, mine, _ = kinds[what]
        part = pl.ds(0, n - 1)
        return copy(
            src.at[part], dst.at[part], what, slots[what, key, scatter], lax.rem(mine + 1, n)
        )

    started = []

    for load in loads[:3]:
        load.wait()
    a = a_in[...]
    b = b_in[...]
    ag_a[0, col] = a.astype(BF16)
    ag_b[row] = b.astype(BF16)

    pl.semaphore_wait(barrier, n_row + n_col - 2)
    start("b", 0, False, ag_b, ag_b)
    start("a", 0, False, ag_a.at[0], ag_a.at[0])

    for load in loads[3:]:
        load.wait()
    for i, ref in enumerate((c_in, mc_in, vc_in)):
        for d in range(n_all):
            g, h = d // groups, d % groups
            split[i, d] = ref[g * chunk : (g + 1) * chunk, h * LANES : (h + 1) * LANES]
    st_a[0], st_a[1], st_a[2] = a, ma_in[...], va_in[...]
    st_b[0], st_b[1], st_b[2] = b, mb_in[...], vb_in[...]
    st_c[0], st_c[1], st_c[2] = split[0, me], split[1, me], split[2, me]
    c_b[...] = c_in[...].astype(BF16)
    load_x.wait()
    load_k.wait()

    def act(m):
        x = x_s[...].reshape(tile_rows * depth, tile_cols).astype(F32)
        huber = jnp.clip(m - x, -1.0, 1.0)
        logit = 0.5 * jnp.tanh(0.5 * m) + jnp.where(x > 0, -0.5, 0.5)
        is_logit = jnp.broadcast_to(kind_s[0:1, :], m.shape) == 1
        y_s[...] = jnp.where(is_logit, logit, huber).astype(BF16)

    def product(p, b):
        return lax.dot_general(p, b, (((1,), (1,)), ((), ())), preferred_element_type=F32)

    spread = learn_rate * ITERS
    for it in range(ITERS):
        last = it == ITERS - 1
        counter = STEP + it + 1

        whole("a", it, False, ag_a.at[it], ag_a.at[it]).wait_recv()
        a_b[...] = ag_a[it].reshape(tile_rows, rank)
        a_f[...] = a_b[...].astype(F32)
        if it > 0:
            whole("c", it, False, ag_c.at[it], ag_c.at[it]).wait_recv()
            for d in range(n_all):
                g, h = d // groups, d % groups
                c_b[g * chunk : (g + 1) * chunk, h * LANES : (h + 1) * LANES] = ag_c[it, d]
        c_f[...] = c_b[...].astype(F32)

        def scale_rows(s, carry):
            at = pl.ds(pl.multiple_of(s * P_ROWS, P_ROWS), P_ROWS)
            span = pl.ds(pl.multiple_of(s * P_ROWS * depth, P_ROWS * depth), P_ROWS * depth)
            p = a_b[at, :][:, None, :] * c_b[...][None]
            p_s[span, :] = p.reshape(P_ROWS * depth, rank)
            return carry

        lax.fori_loop(0, tile_rows // P_ROWS, scale_rows, 0)

        if it == 0:
            whole("b", 0, False, ag_b, ag_b).wait_recv()
            bh = ag_b[...].reshape(tile_cols, rank)
            act(product(p_s[...], bh))
        else:
            for h in range(HALVES):
                whole("b", (it, h), False, ag_bh.at[it, h], ag_bh.at[it, h]).wait_recv()
                m = product(
                    p_s[:, h * half : (h + 1) * half], ag_bh[it, h].reshape(tile_cols, half)
                )
                if h > 0:
                    m = m_s[...] + m
                if h < HALVES - 1:
                    m_s[...] = m
                else:
                    act(m)
            bh = jnp.concatenate(
                [ag_bh[it, h].reshape(tile_cols, half) for h in range(HALVES)], axis=1
            )

        gc[...] = jnp.zeros_like(gc)

        def project(s, carry):
            at = pl.ds(pl.multiple_of(s * Z_ROWS, Z_ROWS), Z_ROWS)
            span = pl.ds(pl.multiple_of(s * Z_ROWS * depth, Z_ROWS * depth), Z_ROWS * depth)
            z = jnp.dot(y_s[span, :], bh, preferred_element_type=F32)
            z = z.reshape(Z_ROWS, depth, rank)
            ga[at, :] = jnp.sum(z * c_f[...][None], axis=1) * scales[0]
            gc[...] += jnp.sum(z * a_f[at, :][:, None, :], axis=0)
            return carry

        lax.fori_loop(0, tile_rows // Z_ROWS, project, 0)

        for d in range(n_all):
            g, h = d // groups, d % groups
            gs_c[it, d] = (
                gc[g * chunk : (g + 1) * chunk, h * LANES : (h + 1) * LANES] * scales[2]
            ).astype(BF16)
        start("c", it, True, gs_c.at[it], rs_c.at[it])
        rs_c[it, me] = gs_c[it, me]
        gs_a[it] = ga[...].astype(BF16).reshape(n_col, own_a, rank)
        start("a", it, True, gs_a.at[it], rs_a.at[it])

        for h in range(HALVES):
            cut = slice(h * half, (h + 1) * half)
            g = lax.dot_general(
                y_s[...], p_s[:, cut], (((0,), (0,)), ((), ())), preferred_element_type=F32
            ) * scales[1]
            gb[:, cut] = g
            gs_b[it, h] = g.astype(BF16).reshape(n_row, own_b, half)
            start("b", (it, h), True, gs_b.at[it, h], rs_b.at[it, h])

        whole("a", it, True, gs_a.at[it], rs_a.at[it]).wait_recv()
        grad = ga[pl.ds(pl.multiple_of(col * own_a, own_a), own_a), :]
        for k in range(1, n_col):
            grad = grad + rs_a[it, lax.rem(col + k, n_col)].astype(F32)
        st_a[0], st_a[1], st_a[2] = adam_step(st_a[0], st_a[1], st_a[2], grad, counter)
        if last:
            out_a[...] = (a_in[...] - st_a[0]) / spread
            put_a = pltpu.make_async_copy(out_a, oa, out_sem.at[0])
            put_a.start()
        else:
            ag_a[it + 1, col] = st_a[0].astype(BF16)
            start("a", it + 1, False, ag_a.at[it + 1], ag_a.at[it + 1])

        whole("c", it, True, gs_c.at[it], rs_c.at[it]).wait_recv()
        st_c[0], st_c[1], st_c[2] = adam_step(
            st_c[0], st_c[1], st_c[2], jnp.sum(rs_c[it].astype(F32), axis=0), counter
        )
        c = (split[0, me] - st_c[0]) / spread if last else st_c[0]
        ag_c[it + 1, me] = c.astype(BF16)
        start("c", it + 1, False, ag_c.at[it + 1], ag_c.at[it + 1])

        for h in range(HALVES):
            cut = slice(h * half, (h + 1) * half)
            whole("b", (it, h), True, gs_b.at[it, h], rs_b.at[it, h]).wait_recv()
            grad = gb[pl.ds(pl.multiple_of(row * own_b, own_b), own_b), cut]
            for k in range(1, n_row):
                grad = grad + rs_b[it, h, lax.rem(row + k, n_row)].astype(F32)
            f, m, v = adam_step(st_b[0, :, cut], st_b[1, :, cut], st_b[2, :, cut], grad, counter)
            if last:
                out_b[:, cut] = (b_in[:, cut] - f) / spread
            else:
                st_b[0, :, cut], st_b[1, :, cut], st_b[2, :, cut] = f, m, v
                ag_bh[it + 1, h, row] = f.astype(BF16)
                start("b", (it + 1, h), False, ag_bh.at[it + 1, h], ag_bh.at[it + 1, h])
        if last:
            put_b = pltpu.make_async_copy(out_b, ob, out_sem.at[1])
            put_b.start()

    whole("c", ITERS, False, ag_c.at[ITERS], ag_c.at[ITERS]).wait_recv()
    for d in range(n_all):
        g, h = d // groups, d % groups
        out_c[g * chunk : (g + 1) * chunk, h * LANES : (h + 1) * LANES] = ag_c[ITERS, d].astype(F32)
    put_c = pltpu.make_async_copy(out_c, oc, out_sem.at[2])
    put_c.start()
    for args in started:
        whole(*args).wait_send()
    for put in (put_a, put_b, put_c):
        put.wait()


def hand_on(a, b, c, oa, ob, oc, sems):
    moves = [
        pltpu.make_async_copy(src, dst, sems.at[i])
        for i, (src, dst) in enumerate(((a, oa), (b, ob), (c, oc)))
    ]
    for move in moves:
        move.start()
    for move in moves:
        move.wait()


def shards(tensor, loss_kind, a, b, c, ma, va, mb, vb, mc, vc):
    tile_rows, depth, tile_cols = tensor.shape
    rank = a.shape[1]
    half = rank // HALVES
    n_row = lax.axis_size("row")
    n_col = lax.axis_size("col")
    n_all = n_row * n_col
    full_rows = tile_rows * n_row
    full_cols = tile_cols * n_col
    scales = (
        1.0 / math.sqrt(full_cols * depth),
        1.0 / math.sqrt(full_rows * depth),
        1.0 / math.sqrt(full_rows * full_cols),
    )
    chunk = depth * rank // (n_all * LANES)
    own_a, own_b = a.shape[0], b.shape[0]
    hbm = pl.BlockSpec(memory_space=pl.ANY)
    slots = ITERS * (4 + 2 * HALVES) + 2
    outs = pl.pallas_call(
        functools.partial(kernel, n_row, n_col, scales),
        out_shape=tuple(jax.ShapeDtypeStruct(f.shape, F32) for f in (a, b, c)),
        in_specs=[hbm] * 11,
        out_specs=[hbm] * 3,
        scratch_shapes=[
            pltpu.VMEM(tensor.shape, tensor.dtype),
            pltpu.VMEM((8, tile_cols), jnp.int32),
            pltpu.VMEM((ITERS, n_col, own_a, rank), BF16),
            pltpu.VMEM((n_row, own_b, rank), BF16),
            pltpu.VMEM((ITERS, HALVES, n_row, own_b, half), BF16),
            pltpu.VMEM((ITERS + 1, n_all, chunk, LANES), BF16),
            pltpu.VMEM((ITERS, n_col, own_a, rank), BF16),
            pltpu.VMEM((ITERS, HALVES, n_row, own_b, half), BF16),
            pltpu.VMEM((ITERS, n_all, chunk, LANES), BF16),
            pltpu.VMEM((ITERS, n_col, own_a, rank), BF16),
            pltpu.VMEM((ITERS, HALVES, n_row, own_b, half), BF16),
            pltpu.VMEM((ITERS, n_all, chunk, LANES), BF16),
            pltpu.VMEM((tile_rows, rank), BF16),
            pltpu.VMEM((tile_rows, rank), F32),
            pltpu.VMEM((depth, rank), BF16),
            pltpu.VMEM((depth, rank), F32),
            pltpu.VMEM((tile_rows, rank), F32),
            pltpu.VMEM((tile_cols, rank), F32),
            pltpu.VMEM((depth, rank), F32),
            pltpu.VMEM((3, own_a, rank), F32),
            pltpu.VMEM((3, own_b, rank), F32),
            pltpu.VMEM((3, chunk, LANES), F32),
            pltpu.VMEM((3, n_all, chunk, LANES), F32),
            pltpu.VMEM((tile_rows * depth, rank), BF16),
            pltpu.VMEM((tile_rows * depth, tile_cols), BF16),
            pltpu.VMEM((tile_rows * depth, tile_cols), F32),
            *[pltpu.VMEM(f.shape, F32) for f in (a, b, c)],
            *[pltpu.VMEM(f.shape, F32) for f in (a, b, c, ma, va, mb, vb, mc, vc)],
            pltpu.SemaphoreType.DMA((11,)),
            pltpu.SemaphoreType.DMA((slots,)),
            pltpu.SemaphoreType.DMA((slots,)),
            pltpu.SemaphoreType.DMA((3,)),
        ],
        compiler_params=pltpu.CompilerParams(
            collective_id=0, has_side_effects=True, vmem_limit_bytes=60 * 1024 * 1024
        ),
    )(tensor, loss_kind, a, b, c, ma, va, mb, vb, mc, vc)
    return pl.pallas_call(
        hand_on,
        out_shape=tuple(jax.ShapeDtypeStruct(f.shape, F32) for f in (a, b, c)),
        in_specs=[hbm] * 3,
        out_specs=[hbm] * 3,
        scratch_shapes=[pltpu.SemaphoreType.DMA((3,))],
    )(*outs)


def solution(mesh):
    in_specs = (
        P("row", None, "col"),
        P("row", None, "col"),
        P(("row", "col"), None),
        P(("col", "row"), None),
        P(),
        P(("row", "col"), None),
        P(("row", "col"), None),
        P(("col", "row"), None),
        P(("col", "row"), None),
        P(),
        P(),
    )
    out_specs = (P(("row", "col"), None), P(("col", "row"), None), P())
    return jax.shard_map(shards, mesh=mesh, in_specs=in_specs, out_specs=out_specs, check_vma=False)
```

time: 54.7 us -> 54.7 us (level)
    pallas_call x1, Pallas kernels: 52.3 us -> 45.7 us  [shards(): pl.pallas_call(functools.partial(kernel, n_row, n_col, scales), out_shape...]
    pallas_call x1, Pallas kernels: 1.65 us -> 8.08 us  [shards(): pl.pallas_call(hand_on, out_shape=tuple((jax.ShapeDtypeStruct(f.shape, F3...]
where the time goes in v1:
time: 54.7 us; the launch traced here: 54.6 us
  Pallas kernels  53.8 us (98%)
  between operations  0.8 us (1%)
    pallas_call x1, Pallas kernels, shards(): pl.pallas_call(functools.partial(kernel, n_row, n_col, scales), out_shape...  45.7 us
    pallas_call x1, Pallas kernels, shards(): pl.pallas_call(hand_on, out_shape=tuple((jax.ShapeDtypeStruct(f.shape, F3...  8.08 us

profile of v1, /device:TPU:0, one launch (start us, length us, event | category | flops | bytes accessed | tf_op | source)
XLA Modules:
  0.0 54.6 jit_solution(6934024312811851530)
XLA Ops:
  0.6 45.7 %shard_map.130 = (f32[32,512]{1,0:T(8,128)}, f32[16,512]{1,0:T(8,128)}, f32[64,512]{1,0:T(8,128)}) custom-call(bf16[128,64,128]{2,1,0:T(8,128)(2,1)} %tensor.1, s32[128,64,128]{2,1,0:T(8,128)} %kind.1, f32[32,512]{1,0:T(8,128)} %a_hbm.1, f32[16,512]{1,0:T(8,128)} %b_hbm.1, f32[64,512]{1,0:T(8,128)} %c_hbm.1, f32[32,512]{1,0:T(8,128)} %ma_hbm.1, ...), custom_call_target="tpu_custom_call" | custom-call | tf_op jit(solution)/shard_map/pallas_call | solution.py:313
  46.3 8.1 %shard_map.131 = (f32[32,512]{1,0:T(8,128)}, f32[16,512]{1,0:T(8,128)}, f32[64,512]{1,0:T(8,128)}) custom-call(f32[32,512]{1,0:T(8,128)} %get-tuple-element.6.a, f32[16,512]{1,0:T(8,128)} %get-tuple-element.7.b, f32[64,512]{1,0:T(8,128)} %get-tuple-element.8.c), custom_call_target="tpu_custom_call" | custom-call | tf_op jit(solution)/shard_map/pallas_call | solution.py:356

commit v2 on v1

--- a/solution.py
+++ b/solution.py
@@ -12,7 +12,7 @@
 STEP = 10
 HALVES = 2
 P_ROWS = 16
-Z_ROWS = 64
+ROWS = 16
 LANES = 128
 
 learn_rate = 0.05
@@ -38,7 +38,7 @@
     tensor, kind, a_hbm, b_hbm, c_hbm, ma_hbm, va_hbm, mb_hbm, vb_hbm, mc_hbm, vc_hbm,
     oa, ob, oc,
     x_s, kind_s, ag_a, ag_b, ag_bh, ag_c, gs_a, gs_b, gs_c, rs_a, rs_b, rs_c,
-    a_b, a_f, c_b, c_f, ga, gb, gc, st_a, st_b, st_c, split, p_s, y_s, m_s, out_a, out_b, out_c,
+    a_b, a_f, c_b, c_f, ga, gb, gc, st_a, st_b, st_c, split, p_s, y_s, out_a, out_b, out_c,
     a_in, b_in, c_in, ma_in, va_in, mb_in, vb_in, mc_in, vc_in,
     load_sem, sends, recvs, out_sem,
 ):
@@ -145,12 +145,12 @@
     load_x.wait()
     load_k.wait()
 
-    def act(m):
-        x = x_s[...].reshape(tile_rows * depth, tile_cols).astype(F32)
+    def act(m, rows):
+        x = x_s[rows].reshape(m.shape).astype(F32)
         huber = jnp.clip(m - x, -1.0, 1.0)
         logit = 0.5 * jnp.tanh(0.5 * m) + jnp.where(x > 0, -0.5, 0.5)
         is_logit = jnp.broadcast_to(kind_s[0:1, :], m.shape) == 1
-        y_s[...] = jnp.where(is_logit, logit, huber).astype(BF16)
+        return jnp.where(is_logit, logit, huber).astype(BF16)
 
     def product(p, b):
         return lax.dot_general(p, b, (((1,), (1,)), ((), ())), preferred_element_type=F32)
@@ -170,47 +170,46 @@
                 c_b[g * chunk : (g + 1) * chunk, h * LANES : (h + 1) * LANES] = ag_c[it, d]
         c_f[...] = c_b[...].astype(F32)
 
-        def scale_rows(s, carry):
-            at = pl.ds(pl.multiple_of(s * P_ROWS, P_ROWS), P_ROWS)
-            span = pl.ds(pl.multiple_of(s * P_ROWS * depth, P_ROWS * depth), P_ROWS * depth)
-            p = a_b[at, :][:, None, :] * c_b[...][None]
-            p_s[span, :] = p.reshape(P_ROWS * depth, rank)
-            return carry
-
-        lax.fori_loop(0, tile_rows // P_ROWS, scale_rows, 0)
-
         if it == 0:
+
+            def scale_rows(s, carry):
+                at = pl.ds(pl.multiple_of(s * P_ROWS, P_ROWS), P_ROWS)
+                span = pl.ds(pl.multiple_of(s * P_ROWS * depth, P_ROWS * depth), P_ROWS * depth)
+                p = a_b[at, :][:, None, :] * c_b[...][None]
+                p_s[span, :] = p.reshape(P_ROWS * depth, rank)
+                return carry
+
+            lax.fori_loop(0, tile_rows // P_ROWS, scale_rows, 0)
             whole("b", 0, False, ag_b, ag_b).wait_recv()
-            bh = ag_b[...].reshape(tile_cols, rank)
-            act(product(p_s[...], bh))
+            b_f = ag_b[...].reshape(tile_cols, rank)
         else:
             for h in range(HALVES):
                 whole("b", (it, h), False, ag_bh.at[it, h], ag_bh.at[it, h]).wait_recv()
-                m = product(
-                    p_s[:, h * half : (h + 1) * half], ag_bh[it, h].reshape(tile_cols, half)
-                )
-                if h > 0:
-                    m = m_s[...] + m
-                if h < HALVES - 1:
-                    m_s[...] = m
-                else:
-                    act(m)
-            bh = jnp.concatenate(
+            b_f = jnp.concatenate(
                 [ag_bh[it, h].reshape(tile_cols, half) for h in range(HALVES)], axis=1
             )
 
-        gc[...] = jnp.zeros_like(gc)
-
-        def project(s, carry):
-            at = pl.ds(pl.multiple_of(s * Z_ROWS, Z_ROWS), Z_ROWS)
-            span = pl.ds(pl.multiple_of(s * Z_ROWS * depth, Z_ROWS * depth), Z_ROWS * depth)
-            z = jnp.dot(y_s[span, :], bh, preferred_element_type=F32)
-            z = z.reshape(Z_ROWS, depth, rank)
-            ga[at, :] = jnp.sum(z * c_f[...][None], axis=1) * scales[0]
-            gc[...] += jnp.sum(z * a_f[at, :][:, None, :], axis=0)
-            return carry
-
-        lax.fori_loop(0, tile_rows // Z_ROWS, project, 0)
+        def forward(s):
+            rows = slice(s * ROWS, (s + 1) * ROWS)
+            span = slice(s * ROWS * depth, (s + 1) * ROWS * depth)
+            if it > 0:
+                p = a_b[rows, :][:, None, :] * c_b[...][None]
+                p_s[span, :] = p.reshape(ROWS * depth, rank)
+            y = act(product(p_s[span, :], b_f), rows)
+            y_s[span, :] = y
+            return y
+
+        steps = tile_rows // ROWS
+        later = forward(0)
+        for s in range(steps):
+            y = later
+            if s < steps - 1:
+                later = forward(s + 1)
+            rows = slice(s * ROWS, (s + 1) * ROWS)
+            z = jnp.dot(y, b_f, preferred_element_type=F32).reshape(ROWS, depth, rank)
+            ga[rows, :] = jnp.sum(z * c_f[...][None], axis=1) * scales[0]
+            part = jnp.sum(z * a_f[rows, :][:, None, :], axis=0)
+            gc[...] = part if s == 0 else gc[...] + part
 
         for d in range(n_all):
             g, h = d // groups, d % groups
@@ -281,15 +280,10 @@
         put.wait()
 
 
-def hand_on(a, b, c, oa, ob, oc, sems):
-    moves = [
-        pltpu.make_async_copy(src, dst, sems.at[i])
-        for i, (src, dst) in enumerate(((a, oa), (b, ob), (c, oc)))
-    ]
-    for move in moves:
-        move.start()
-    for move in moves:
-        move.wait()
+def hand_on(a, b, c, oa, ob, oc):
+    oa[...] = a[...]
+    ob[...] = b[...]
+    oc[...] = c[...]
 
 
 def shards(tensor, loss_kind, a, b, c, ma, va, mb, vb, mc, vc):
@@ -341,7 +335,6 @@
             pltpu.VMEM((3, n_all, chunk, LANES), F32),
             pltpu.VMEM((tile_rows * depth, rank), BF16),
             pltpu.VMEM((tile_rows * depth, tile_cols), BF16),
-            pltpu.VMEM((tile_rows * depth, tile_cols), F32),
             *[pltpu.VMEM(f.shape, F32) for f in (a, b, c)],
             *[pltpu.VMEM(f.shape, F32) for f in (a, b, c, ma, va, mb, vb, mc, vc)],
             pltpu.SemaphoreType.DMA((11,)),
@@ -353,12 +346,12 @@
             collective_id=0, has_side_effects=True, vmem_limit_bytes=60 * 1024 * 1024
         ),
     )(tensor, loss_kind, a, b, c, ma, va, mb, vb, mc, vc)
+    vmem = pl.BlockSpec(memory_space=pltpu.VMEM)
     return pl.pallas_call(
         hand_on,
         out_shape=tuple(jax.ShapeDtypeStruct(f.shape, F32) for f in (a, b, c)),
-        in_specs=[hbm] * 3,
-        out_specs=[hbm] * 3,
-        scratch_shapes=[pltpu.SemaphoreType.DMA((3,))],
+        in_specs=[vmem] * 3,
+        out_specs=[vmem] * 3,
     )(*outs)
 
 

time: 54.7 us -> 45.9 us (0.84)
  Pallas kernels: 53.8 us -> 45.1 us
    pallas_call x1, Pallas kernels: 8.08 us -> 1.65 us  [shards(): pl.pallas_call(hand_on, out_shape=tuple((jax.ShapeDtypeStruct(f.shape, F3...]
    pallas_call x1, Pallas kernels: 45.7 us -> 43.5 us  [shards(): pl.pallas_call(functools.partial(kernel, n_row, n_col, scales), out_shape...]
where the time goes in v2:
time: 45.9 us; the launch traced here: 45.8 us
  Pallas kernels  45.1 us (98%)
  between operations  0.64 us (1%)
    pallas_call x1, Pallas kernels, shards(): pl.pallas_call(functools.partial(kernel, n_row, n_col, scales), out_shape...  43.5 us
    pallas_call x1, Pallas kernels, shards(): pl.pallas_call(hand_on, out_shape=tuple((jax.ShapeDtypeStruct(f.shape, F3...  1.65 us

profile of v2, /device:TPU:0, one launch (start us, length us, event | category | flops | bytes accessed | tf_op | source)
XLA Modules:
  0.0 45.8 jit_solution(10342968032093989314)
XLA Ops:
  0.6 43.5 %shard_map.130 = (f32[32,512]{1,0:T(8,128)}, f32[16,512]{1,0:T(8,128)}, f32[64,512]{1,0:T(8,128)}) custom-call(bf16[128,64,128]{2,1,0:T(8,128)(2,1)} %tensor.1, s32[128,64,128]{2,1,0:T(8,128)} %kind.1, f32[32,512]{1,0:T(8,128)} %a_hbm.1, f32[16,512]{1,0:T(8,128)} %b_hbm.1, f32[64,512]{1,0:T(8,128)} %c_hbm.1, f32[32,512]{1,0:T(8,128)} %ma_hbm.1, ...), custom_call_target="tpu_custom_call" | custom-call | tf_op jit(solution)/shard_map/pallas_call | solution.py:307
  44.1 1.7 %shard_map.131 = (f32[32,512]{1,0:T(8,128)}, f32[16,512]{1,0:T(8,128)}, f32[64,512]{1,0:T(8,128)}) custom-call(f32[32,512]{1,0:T(8,128)} %get-tuple-element.6.a, f32[16,512]{1,0:T(8,128)} %get-tuple-element.7.b, f32[64,512]{1,0:T(8,128)} %get-tuple-element.8.c), custom_call_target="tpu_custom_call" | custom-call | tf_op jit(solution)/shard_map/pallas_call | solution.py:350

commit v3 on v2

--- a/solution.py
+++ b/solution.py
@@ -10,7 +10,7 @@
 
 ITERS = 2
 STEP = 10
-HALVES = 2
+HALVES = 1
 P_ROWS = 16
 ROWS = 16
 LANES = 128
@@ -38,7 +38,7 @@
     tensor, kind, a_hbm, b_hbm, c_hbm, ma_hbm, va_hbm, mb_hbm, vb_hbm, mc_hbm, vc_hbm,
     oa, ob, oc,
     x_s, kind_s, ag_a, ag_b, ag_bh, ag_c, gs_a, gs_b, gs_c, rs_a, rs_b, rs_c,
-    a_b, a_f, c_b, c_f, ga, gb, gc, st_a, st_b, st_c, split, p_s, y_s, out_a, out_b, out_c,
+    a_b, a_f, c_b, c_f, ga, gb, gc, st_a, st_b, st_c, split, p_s, y_s, out_a, out_b,
     a_in, b_in, c_in, ma_in, va_in, mb_in, vb_in, mc_in, vc_in,
     load_sem, sends, recvs, out_sem,
 ):
@@ -73,6 +73,8 @@
         "b": (n_row, row, lambda d: {"row": d}),
         "c": (n_all, me, device),
     }
+    for load in loads[:2]:
+        load.start()
     barrier = pltpu.get_barrier_semaphore()
 
     for what in "ba":
@@ -87,7 +89,7 @@
 
         lax.fori_loop(1, n, greet, 0)
 
-    for load in loads:
+    for load in loads[2:]:
         load.start()
     load_k.start()
     load_x.start()
@@ -121,7 +123,7 @@
 
     started = []
 
-    for load in loads[:3]:
+    for load in loads[:2]:
         load.wait()
     a = a_in[...]
     b = b_in[...]
@@ -132,7 +134,7 @@
     start("b", 0, False, ag_b, ag_b)
     start("a", 0, False, ag_a.at[0], ag_a.at[0])
 
-    for load in loads[3:]:
+    for load in loads[2:]:
         load.wait()
     for i, ref in enumerate((c_in, mc_in, vc_in)):
         for d in range(n_all):
@@ -170,16 +172,16 @@
                 c_b[g * chunk : (g + 1) * chunk, h * LANES : (h + 1) * LANES] = ag_c[it, d]
         c_f[...] = c_b[...].astype(F32)
 
+        def scale_rows(s, carry):
+            at = pl.ds(pl.multiple_of(s * P_ROWS, P_ROWS), P_ROWS)
+            span = pl.ds(pl.multiple_of(s * P_ROWS * depth, P_ROWS * depth), P_ROWS * depth)
+            p = a_b[at, :][:, None, :] * c_b[...][None]
+            p_s[span, :] = p.reshape(P_ROWS * depth, rank)
+            return carry
+
+        lax.fori_loop(0, tile_rows // P_ROWS, scale_rows, 0)
+
         if it == 0:
-
-            def scale_rows(s, carry):
-                at = pl.ds(pl.multiple_of(s * P_ROWS, P_ROWS), P_ROWS)
-                span = pl.ds(pl.multiple_of(s * P_ROWS * depth, P_ROWS * depth), P_ROWS * depth)
-                p = a_b[at, :][:, None, :] * c_b[...][None]
-                p_s[span, :] = p.reshape(P_ROWS * depth, rank)
-                return carry
-
-            lax.fori_loop(0, tile_rows // P_ROWS, scale_rows, 0)
             whole("b", 0, False, ag_b, ag_b).wait_recv()
             b_f = ag_b[...].reshape(tile_cols, rank)
         else:
@@ -192,9 +194,6 @@
         def forward(s):
             rows = slice(s * ROWS, (s + 1) * ROWS)
             span = slice(s * ROWS * depth, (s + 1) * ROWS * depth)
-            if it > 0:
-                p = a_b[rows, :][:, None, :] * c_b[...][None]
-                p_s[span, :] = p.reshape(ROWS * depth, rank)
             y = act(product(p_s[span, :], b_f), rows)
             y_s[span, :] = y
             return y
@@ -218,8 +217,6 @@
             ).astype(BF16)
         start("c", it, True, gs_c.at[it], rs_c.at[it])
         rs_c[it, me] = gs_c[it, me]
-        gs_a[it] = ga[...].astype(BF16).reshape(n_col, own_a, rank)
-        start("a", it, True, gs_a.at[it], rs_a.at[it])
 
         for h in range(HALVES):
             cut = slice(h * half, (h + 1) * half)
@@ -229,6 +226,21 @@
             gb[:, cut] = g
             gs_b[it, h] = g.astype(BF16).reshape(n_row, own_b, half)
             start("b", (it, h), True, gs_b.at[it, h], rs_b.at[it, h])
+
+        gs_a[it] = ga[...].astype(BF16).reshape(n_col, own_a, rank)
+        start("a", it, True, gs_a.at[it], rs_a.at[it])
+
+        whole("c", it, True, gs_c.at[it], rs_c.at[it]).wait_recv()
+        st_c[0], st_c[1], st_c[2] = adam_step(
+            st_c[0], st_c[1], st_c[2], jnp.sum(rs_c[it].astype(F32), axis=0), counter
+        )
+        c = (split[0, me] - st_c[0]) / spread if last else st_c[0]
+        ag_c[it + 1, me] = c.astype(BF16)
+        land = oc if last else ag_c.at[it + 1]
+        start("c", it + 1, False, ag_c.at[it + 1], land)
+        if last:
+            put_c = pltpu.make_async_copy(ag_c.at[it + 1, me], oc.at[me], out_sem.at[2])
+            put_c.start()
 
         whole("a", it, True, gs_a.at[it], rs_a.at[it]).wait_recv()
         grad = ga[pl.ds(pl.multiple_of(col * own_a, own_a), own_a), :]
@@ -242,14 +254,6 @@
         else:
             ag_a[it + 1, col] = st_a[0].astype(BF16)
             start("a", it + 1, False, ag_a.at[it + 1], ag_a.at[it + 1])
-
-        whole("c", it, True, gs_c.at[it], rs_c.at[it]).wait_recv()
-        st_c[0], st_c[1], st_c[2] = adam_step(
-            st_c[0], st_c[1], st_c[2], jnp.sum(rs_c[it].astype(F32), axis=0), counter
-        )
-        c = (split[0, me] - st_c[0]) / spread if last else st_c[0]
-        ag_c[it + 1, me] = c.astype(BF16)
-        start("c", it + 1, False, ag_c.at[it + 1], ag_c.at[it + 1])
 
         for h in range(HALVES):
             cut = slice(h * half, (h + 1) * half)
@@ -268,12 +272,7 @@
             put_b = pltpu.make_async_copy(out_b, ob, out_sem.at[1])
             put_b.start()
 
-    whole("c", ITERS, False, ag_c.at[ITERS], ag_c.at[ITERS]).wait_recv()
-    for d in range(n_all):
-        g, h = d // groups, d % groups
-        out_c[g * chunk : (g + 1) * chunk, h * LANES : (h + 1) * LANES] = ag_c[ITERS, d].astype(F32)
-    put_c = pltpu.make_async_copy(out_c, oc, out_sem.at[2])
-    put_c.start()
+    whole("c", ITERS, False, ag_c.at[ITERS], oc).wait_recv()
     for args in started:
         whole(*args).wait_send()
     for put in (put_a, put_b, put_c):
@@ -283,7 +282,11 @@
 def hand_on(a, b, c, oa, ob, oc):
     oa[...] = a[...]
     ob[...] = b[...]
-    oc[...] = c[...]
+    chunk = c.shape[1]
+    groups = oc.shape[1] // LANES
+    for d in range(c.shape[0]):
+        g, h = d // groups, d % groups
+        oc[g * chunk : (g + 1) * chunk, h * LANES : (h + 1) * LANES] = c[d].astype(F32)
 
 
 def shards(tensor, loss_kind, a, b, c, ma, va, mb, vb, mc, vc):
@@ -306,7 +309,11 @@
     slots = ITERS * (4 + 2 * HALVES) + 2
     outs = pl.pallas_call(
         functools.partial(kernel, n_row, n_col, scales),
-        out_shape=tuple(jax.ShapeDtypeStruct(f.shape, F32) for f in (a, b, c)),
+        out_shape=(
+            jax.ShapeDtypeStruct(a.shape, F32),
+            jax.ShapeDtypeStruct(b.shape, F32),
+            jax.ShapeDtypeStruct((n_all, chunk, LANES), BF16),
+        ),
         in_specs=[hbm] * 11,
         out_specs=[hbm] * 3,
         scratch_shapes=[
@@ -335,7 +342,7 @@
             pltpu.VMEM((3, n_all, chunk, LANES), F32),
             pltpu.VMEM((tile_rows * depth, rank), BF16),
             pltpu.VMEM((tile_rows * depth, tile_cols), BF16),
-            *[pltpu.VMEM(f.shape, F32) for f in (a, b, c)],
+            *[pltpu.VMEM(f.shape, F32) for f in (a, b)],
             *[pltpu.VMEM(f.shape, F32) for f in (a, b, c, ma, va, mb, vb, mc, vc)],
             pltpu.SemaphoreType.DMA((11,)),
             pltpu.SemaphoreType.DMA((slots,)),

time: 45.9 us -> 44.5 us (0.969)
  Pallas kernels: 45.1 us -> 43.7 us
    pallas_call x1, Pallas kernels: 43.5 us -> 42.1 us  [shards(): pl.pallas_call(functools.partial(kernel, n_row, n_col, scales), out_shape...]
where the time goes in v3:
time: 44.5 us; the launch traced here: 44.3 us
  Pallas kernels  43.7 us (98%)
  between operations  0.64 us (1%)
    pallas_call x1, Pallas kernels, shards(): pl.pallas_call(functools.partial(kernel, n_row, n_col, scales), out_shape...  42.1 us
    pallas_call x1, Pallas kernels, shards(): pl.pallas_call(hand_on, out_shape=tuple((jax.ShapeDtypeStruct(f.shape, F3...  1.58 us

profile of v3, /device:TPU:0, one launch (start us, length us, event | category | flops | bytes accessed | tf_op | source)
XLA Modules:
  0.0 44.3 jit_solution(16135991941086537045)
XLA Ops:
  0.6 42.1 %shard_map.130 = (f32[32,512]{1,0:T(8,128)}, f32[16,512]{1,0:T(8,128)}, bf16[32,8,128]{2,1,0:T(8,128)(2,1)}) custom-call(bf16[128,64,128]{2,1,0:T(8,128)(2,1)} %tensor.1, s32[128,64,128]{2,1,0:T(8,128)} %kind.1, f32[32,512]{1,0:T(8,128)} %a_hbm.1, f32[16,512]{1,0:T(8,128)} %b_hbm.1, f32[64,512]{1,0:T(8,128)} %c_hbm.1, f32[32,512]{1,0:T(8,128)} %ma_hbm.1, ...), custom_call_target="tpu_custom_call" | custom-call | tf_op jit(solution)/shard_map/pallas_call | solution.py:310
  42.7 1.6 %shard_map.131 = (f32[32,512]{1,0:T(8,128)}, f32[16,512]{1,0:T(8,128)}, f32[64,512]{1,0:T(8,128)}) custom-call(f32[32,512]{1,0:T(8,128)} %get-tuple-element.6.a, f32[16,512]{1,0:T(8,128)} %get-tuple-element.7.b, bf16[32,8,128]{2,1,0:T(8,128)(2,1)} %get-tuple-element.8.c), custom_call_target="tpu_custom_call" | custom-call | tf_op jit(solution)/shard_map/pallas_call | solution.py:357

commit v4 on v3

--- a/solution.py
+++ b/solution.py
@@ -12,7 +12,9 @@
 STEP = 10
 HALVES = 1
 P_ROWS = 16
-ROWS = 16
+DEEP = 8
+TURN = 4
+PAD = 8
 LANES = 128
 
 learn_rate = 0.05
@@ -37,8 +39,8 @@
     n_row, n_col, scales,
     tensor, kind, a_hbm, b_hbm, c_hbm, ma_hbm, va_hbm, mb_hbm, vb_hbm, mc_hbm, vc_hbm,
     oa, ob, oc,
-    x_s, kind_s, ag_a, ag_b, ag_bh, ag_c, gs_a, gs_b, gs_c, rs_a, rs_b, rs_c,
-    a_b, a_f, c_b, c_f, ga, gb, gc, st_a, st_b, st_c, split, p_s, y_s, out_a, out_b,
+    x_s, x_f, x_t, kind_s, ag_a, ag_b, ag_bh, ag_c, gs_a, gs_b, gs_c, rs_a, rs_b, rs_c,
+    a_b, a_f, c_b, c_f, ga, gb, st_a, st_b, st_c, split, p_s, y_s, out_a, out_b,
     a_in, b_in, c_in, ma_in, va_in, mb_in, vb_in, mc_in, vc_in,
     load_sem, sends, recvs, out_sem,
 ):
@@ -147,8 +149,39 @@
     load_x.wait()
     load_k.wait()
 
-    def act(m, rows):
-        x = x_s[rows].reshape(m.shape).astype(F32)
+    pitch = x_f.shape[0] // tile_rows
+
+    def widen(s, carry):
+        for u in range(P_ROWS):
+            i = s * P_ROWS + u
+            x_f[pl.ds(pl.multiple_of(i * pitch, 8), depth), :] = x_s[i].astype(F32)
+        return carry
+
+    lax.fori_loop(0, tile_rows // P_ROWS, widen, 0)
+
+    def turn(s, carry):
+        for u in range(TURN):
+            k = s * TURN + u
+            x_t[k] = x_f[pl.ds(k, tile_rows, stride=pitch), :].astype(BF16)
+        return carry
+
+    lax.fori_loop(0, depth // TURN, turn, 0)
+
+    steps = depth // DEEP
+    per_step = n_all // steps
+    mine_step = lax.div(me, per_step)
+
+    def step_at(s):
+        if steps & (steps - 1):
+            return lax.rem(mine_step + 1 + s, steps)
+        at = mine_step
+        for bit in (1 << i for i in range(steps.bit_length() - 1)):
+            if (steps - 1 - s) & bit:
+                at = at + bit * (1 - 2 * lax.rem(lax.div(mine_step, bit), 2))
+        return at
+
+    def act(m, x):
+        x = x.astype(F32)
         huber = jnp.clip(m - x, -1.0, 1.0)
         logit = 0.5 * jnp.tanh(0.5 * m) + jnp.where(x > 0, -0.5, 0.5)
         is_logit = jnp.broadcast_to(kind_s[0:1, :], m.shape) == 1
@@ -174,12 +207,12 @@
 
         def scale_rows(s, carry):
             at = pl.ds(pl.multiple_of(s * P_ROWS, P_ROWS), P_ROWS)
-            span = pl.ds(pl.multiple_of(s * P_ROWS * depth, P_ROWS * depth), P_ROWS * depth)
-            p = a_b[at, :][:, None, :] * c_b[...][None]
-            p_s[span, :] = p.reshape(P_ROWS * depth, rank)
+            wide = P_ROWS * tile_rows
+            p = c_b[at, :][:, None, :] * a_b[...][None]
+            p_s[pl.ds(pl.multiple_of(s * wide, wide), wide), :] = p.reshape(wide, rank)
             return carry
 
-        lax.fori_loop(0, tile_rows // P_ROWS, scale_rows, 0)
+        lax.fori_loop(0, depth // P_ROWS, scale_rows, 0)
 
         if it == 0:
             whole("b", 0, False, ag_b, ag_b).wait_recv()
@@ -191,31 +224,41 @@
                 [ag_bh[it, h].reshape(tile_cols, half) for h in range(HALVES)], axis=1
             )
 
-        def forward(s):
-            rows = slice(s * ROWS, (s + 1) * ROWS)
-            span = slice(s * ROWS * depth, (s + 1) * ROWS * depth)
-            y = act(product(p_s[span, :], b_f), rows)
+        wide = DEEP * tile_rows
+
+        def forward(g):
+            span = pl.ds(pl.multiple_of(g * wide, wide), wide)
+            x = x_t[pl.ds(pl.multiple_of(g * DEEP, DEEP), DEEP)].reshape(wide, tile_cols)
+            y = act(product(p_s[span, :], b_f), x)
             y_s[span, :] = y
             return y
 
-        steps = tile_rows // ROWS
-        later = forward(0)
+        slot = slots["c", it, True] = len(slots)
+        started.append(("c", it, True, gs_c.at[it], rs_c.at[it]))
+        later = forward(step_at(0))
         for s in range(steps):
+            g = step_at(s)
             y = later
             if s < steps - 1:
-                later = forward(s + 1)
-            rows = slice(s * ROWS, (s + 1) * ROWS)
-            z = jnp.dot(y, b_f, preferred_element_type=F32).reshape(ROWS, depth, rank)
-            ga[rows, :] = jnp.sum(z * c_f[...][None], axis=1) * scales[0]
-            part = jnp.sum(z * a_f[rows, :][:, None, :], axis=0)
-            gc[...] = part if s == 0 else gc[...] + part
-
-        for d in range(n_all):
-            g, h = d // groups, d % groups
-            gs_c[it, d] = (
-                gc[g * chunk : (g + 1) * chunk, h * LANES : (h + 1) * LANES] * scales[2]
-            ).astype(BF16)
-        start("c", it, True, gs_c.at[it], rs_c.at[it])
+                later = forward(step_at(s + 1))
+            z = jnp.dot(y, b_f, preferred_element_type=F32).reshape(DEEP, tile_rows, rank)
+            c_rows = c_f[pl.ds(pl.multiple_of(g * DEEP, DEEP), DEEP), :]
+            part = jnp.sum(z * c_rows[:, None, :], axis=0)
+            ga[...] = part if s == 0 else ga[...] + part
+            part = (jnp.sum(z * a_f[...][None], axis=1) * scales[2]).astype(BF16)
+            for q in range(per_step):
+                u, h = q // groups, q % groups
+                gs_c[it, g * per_step + q] = part[
+                    u * chunk : (u + 1) * chunk, h * LANES : (h + 1) * LANES
+                ]
+            for t in range(steps // 2) if s == steps // 2 else range(steps // 2, steps) if s == steps - 1 else ():
+                far = step_at(t)
+                for q in range(per_step):
+                    if t == steps - 1 and q == 0:
+                        continue
+                    peer = far * per_step + lax.rem(me - mine_step * per_step + q, per_step)
+                    copy(gs_c.at[it, peer], rs_c.at[it, me], "c", slot, peer).start()
+
         rs_c[it, me] = gs_c[it, me]
 
         for h in range(HALVES):
@@ -227,6 +270,7 @@
             gs_b[it, h] = g.astype(BF16).reshape(n_row, own_b, half)
             start("b", (it, h), True, gs_b.at[it, h], rs_b.at[it, h])
 
+        ga[...] = ga[...] * scales[0]
         gs_a[it] = ga[...].astype(BF16).reshape(n_col, own_a, rank)
         start("a", it, True, gs_a.at[it], rs_a.at[it])
 
@@ -318,6 +362,8 @@
         out_specs=[hbm] * 3,
         scratch_shapes=[
             pltpu.VMEM(tensor.shape, tensor.dtype),
+            pltpu.VMEM((tile_rows * (depth + PAD) + depth, tile_cols), F32),
+            pltpu.VMEM((depth, tile_rows, tile_cols), tensor.dtype),
             pltpu.VMEM((8, tile_cols), jnp.int32),
             pltpu.VMEM((ITERS, n_col, own_a, rank), BF16),
             pltpu.VMEM((n_row, own_b, rank), BF16),
@@ -335,7 +381,6 @@
             pltpu.VMEM((depth, rank), F32),
             pltpu.VMEM((tile_rows, rank), F32),
             pltpu.VMEM((tile_cols, rank), F32),
-            pltpu.VMEM((depth, rank), F32),
             pltpu.VMEM((3, own_a, rank), F32),
             pltpu.VMEM((3, own_b, rank), F32),
             pltpu.VMEM((3, chunk, LANES), F32),

time: 44.5 us -> 42 us (0.944)
  Pallas kernels: 43.7 us -> 41.2 us
    pallas_call x1, Pallas kernels: 42.1 us -> 39.6 us  [shards(): pl.pallas_call(functools.partial(kernel, n_row, n_col, scales), out_shape...]
where the time goes in v4:
time: 42 us; the launch traced here: 41.9 us
  Pallas kernels  41.2 us (98%)
  between operations  0.64 us (2%)
    pallas_call x1, Pallas kernels, shards(): pl.pallas_call(functools.partial(kernel, n_row, n_col, scales), out_shape...  39.6 us
    pallas_call x1, Pallas kernels, shards(): pl.pallas_call(hand_on, out_shape=tuple((jax.ShapeDtypeStruct(f.shape, F3...  1.58 us

profile of v4, /device:TPU:0, one launch (start us, length us, event | category | flops | bytes accessed | tf_op | source)
XLA Modules:
  0.0 41.9 jit_solution(14904865553445232254)
XLA Ops:
  0.6 39.6 %shard_map.130 = (f32[32,512]{1,0:T(8,128)}, f32[16,512]{1,0:T(8,128)}, bf16[32,8,128]{2,1,0:T(8,128)(2,1)}) custom-call(bf16[128,64,128]{2,1,0:T(8,128)(2,1)} %tensor.1, s32[128,64,128]{2,1,0:T(8,128)} %kind.1, f32[32,512]{1,0:T(8,128)} %a_hbm.1, f32[16,512]{1,0:T(8,128)} %b_hbm.1, f32[64,512]{1,0:T(8,128)} %c_hbm.1, f32[32,512]{1,0:T(8,128)} %ma_hbm.1, ...), custom_call_target="tpu_custom_call" | custom-call | tf_op jit(solution)/shard_map/pallas_call | solution.py:354
  40.3 1.6 %shard_map.131 = (f32[32,512]{1,0:T(8,128)}, f32[16,512]{1,0:T(8,128)}, f32[64,512]{1,0:T(8,128)}) custom-call(f32[32,512]{1,0:T(8,128)} %get-tuple-element.6.a, f32[16,512]{1,0:T(8,128)} %get-tuple-element.7.b, bf16[32,8,128]{2,1,0:T(8,128)(2,1)} %get-tuple-element.8.c), custom_call_target="tpu_custom_call" | custom-call | tf_op jit(solution)/shard_map/pallas_call | solution.py:402

commit v5 on v4

--- a/solution.py
+++ b/solution.py
@@ -251,7 +251,7 @@
                 gs_c[it, g * per_step + q] = part[
                     u * chunk : (u + 1) * chunk, h * LANES : (h + 1) * LANES
                 ]
-            for t in range(steps // 2) if s == steps // 2 else range(steps // 2, steps) if s == steps - 1 else ():
+            for t in range(steps // 2 + 1) if s == steps // 2 else range(steps // 2 + 1, steps) if s == steps - 1 else ():
                 far = step_at(t)
                 for q in range(per_step):
                     if t == steps - 1 and q == 0:

time: 42 us -> 42.2 us (level)
  no operation moved by 1% of the time
where the time goes in v5:
time: 42.2 us; the launch traced here: 42 us
  Pallas kernels  41.4 us (98%)
  between operations  0.64 us (2%)
    pallas_call x1, Pallas kernels, shards(): pl.pallas_call(functools.partial(kernel, n_row, n_col, scales), out_shape...  39.8 us
    pallas_call x1, Pallas kernels, shards(): pl.pallas_call(hand_on, out_shape=tuple((jax.ShapeDtypeStruct(f.shape, F3...  1.58 us

profile of v5, /device:TPU:0, one launch (start us, length us, event | category | flops | bytes accessed | tf_op | source)
XLA Modules:
  0.0 42.0 jit_solution(7477614309835464967)
XLA Ops:
  0.6 39.8 %shard_map.130 = (f32[32,512]{1,0:T(8,128)}, f32[16,512]{1,0:T(8,128)}, bf16[32,8,128]{2,1,0:T(8,128)(2,1)}) custom-call(bf16[128,64,128]{2,1,0:T(8,128)(2,1)} %tensor.1, s32[128,64,128]{2,1,0:T(8,128)} %kind.1, f32[32,512]{1,0:T(8,128)} %a_hbm.1, f32[16,512]{1,0:T(8,128)} %b_hbm.1, f32[64,512]{1,0:T(8,128)} %c_hbm.1, f32[32,512]{1,0:T(8,128)} %ma_hbm.1, ...), custom_call_target="tpu_custom_call" | custom-call | tf_op jit(solution)/shard_map/pallas_call | solution.py:354
  40.4 1.6 %shard_map.131 = (f32[32,512]{1,0:T(8,128)}, f32[16,512]{1,0:T(8,128)}, f32[64,512]{1,0:T(8,128)}) custom-call(f32[32,512]{1,0:T(8,128)} %get-tuple-element.6.a, f32[16,512]{1,0:T(8,128)} %get-tuple-element.7.b, bf16[32,8,128]{2,1,0:T(8,128)(2,1)} %get-tuple-element.8.c), custom_call_target="tpu_custom_call" | custom-call | tf_op jit(solution)/shard_map/pallas_call | solution.py:402
